TPU v7x, 256 devices: a whole 4x4x8 slice. The times are simulated.
256 devices in a mesh: vol: 64 (over x, z, core), slab: 4 (over y).
Axes of the slice: x: 4, y: 4, z: 8, core: 2. Of those that a mesh axis runs over, the one named last changes fastest.
Arguments:
- face_disp: bfloat16 [64, 524288], P(None, ('vol', 'slab')), may hold values from -6 to 6
- contact_owner: int32 [524288, 1], P(('vol', 'slab')), may hold values from 0 to 63; in each aligned block of 2048 rows (0 to 2047, 2048 to 4095, ...) at most 128 rows name the same one
- segment: int32 [524288], P(('vol', 'slab')), may hold values from 0 to 7
- face_area: float32 [524288], P(('vol', 'slab')), may hold values from 0.5 to 5
- face_nodes: int32 [4, 524288], P(None, ('vol', 'slab')), may hold values from 0 to 1023
- mortar_blocks: bfloat16 [2048, 64, 64], P(('vol', 'slab')), may hold values from -0.75 to 0.75
- gap_offset: bfloat16 [2048, 64], P(('vol', 'slab')), may hold values from -6 to 6
- shape_table: float32 [12, 64], replicated, may hold values from -0.75 to 0.75
- node_disp: float32 [3, 262144], P(None, ('vol', 'slab')), may hold values from -6 to 6
- stiffness: float32 [262144], P(('vol', 'slab')), may hold values from 0.2 to 2
- connect: int32 [8, 262144], P(None, ('vol', 'slab')), may hold values from 0 to 1023
- elem_matrix: float32 [24, 24], replicated, may hold values from -1.25 to 1.25
Outputs:
- residual: float32 [3, 262144], P(None, ('vol', 'slab'))
Inputs may be any that keep to these rules, and one draw needn't show every extreme that they name: `contact_owner`: in each block of 2048 faces no owner index is named by more than 128 faces, and some owner index is named by exactly 128.
All inputs are finite; a program needn't handle non-finite values.
Results may differ from a plain program's by a relative error of at most 0.0028.
Values may be sent and summed in bfloat16 or wider, within the bound.
A program may use at most 64 MiB of HBM per device.

v0:
```python
import functools

import jax
import jax.numpy as jnp
from jax import lax
from jax.experimental import pallas as pl
from jax.experimental.pallas import tpu as pltpu
from jax.sharding import PartitionSpec as P

SH = 256
TILE = 32
GROUP = 4
F32, BF16, I32 = jnp.float32, jnp.bfloat16, jnp.int32
NT = (((1,), (1,)), ((), ()))


def dot(a, b):
    return jnp.dot(a, b, preferred_element_type=F32)


def dot_nt(a, b):
    return lax.dot_general(a, b, NT, preferred_element_type=F32)


def iota(shape, dim):
    return lax.broadcasted_iota(I32, shape, dim)


def hot(mask):
    return jnp.where(mask, 1.0, 0.0).astype(BF16)


def split(value):
    high = value.astype(BF16)
    return high, (value - high.astype(F32)).astype(BF16)


def sort_faces(owner, owners):
    faces = owner.shape[1]
    member = iota((owners, faces), 0) == owner
    member_low = hot(member)
    upto = hot(iota((256, 256), 0) <= iota((256, 256), 1))
    carry = jnp.zeros((owners, 1), F32)
    parts = []
    for k in range(faces // 256):
        part = dot(member_low[:, 256 * k : 256 * k + 256], upto) + carry
        carry = part[:, 255:256]
        parts.append(part)
    rank = jnp.concatenate(parts, axis=1)
    before = hot(iota((owners, owners), 1) < iota((owners, owners), 0))
    count = jnp.broadcast_to(carry, (owners, 128))
    first = dot(before, count.astype(BF16))
    row = jnp.sum(jnp.where(member, rank - 1.0 + first[:, 0:1], 0.0), axis=0, keepdims=True)
    return row.astype(I32), count, first, before


def tile_table(count, first, before):
    owners = count.shape[0]
    tiles = jnp.floor((count + (TILE - 1)) * (1.0 / TILE))
    begin = dot(before, tiles.astype(BF16))
    place = iota((owners, 128), 1).astype(F32)
    inside = (place >= begin) & (place < begin + tiles)
    ids = iota((owners, 128), 0).astype(F32)
    owner = jnp.sum(jnp.where(inside, ids, 0.0), axis=0, keepdims=True)
    start = jnp.sum(jnp.where(inside, first + TILE * (place - begin), 0.0), axis=0, keepdims=True)
    total = jnp.sum(tiles, axis=0, keepdims=True)
    lane = iota((1, 128), 1).astype(F32)
    start = jnp.where(lane < total, start, 2048.0)
    rest = jnp.zeros((5, 128), F32)
    return jnp.concatenate([owner, start, total, rest], axis=0).astype(I32)


def permute(row, disp, segment, area, nodes, sorted_ref):
    faces = row.shape[1]
    nodes_high = nodes >> 7
    area_a = area.astype(BF16)
    area_b, area_c = split(area - area_a.astype(F32))
    extra = jnp.concatenate([(nodes - (nodes_high << 7)).astype(F32), nodes_high.astype(F32)], axis=0).astype(BF16)
    content = jnp.concatenate(
        [
            disp,
            extra,
            area_a,
            area_b,
            area_c,
            jnp.zeros((53, faces), BF16),
            jnp.broadcast_to(segment.astype(F32), (128, faces)).astype(BF16),
        ],
        axis=0,
    )
    for k in range(faces // 256):
        pick = hot(iota((256, faces), 0) + 256 * k == row)
        sorted_ref[256 * k : 256 * k + 256, :] = dot_nt(pick, content)


def high_hot(high_row):
    return iota((8, high_row.shape[1]), 0) == high_row


def elements(node, connect, stiffness, matrix, total_ref, low_ref):
    count = connect.shape[1]
    rows = []
    for c in range(3):
        grid = jnp.concatenate([node[c : c + 1, 128 * h : 128 * h + 128] for h in range(8)], axis=0)
        high, low = split(grid)
        rows += [high.astype(F32), low.astype(F32)]
    table = jnp.concatenate(rows, axis=0).astype(BF16)
    picked, highs = [], []
    for a in range(8):
        index = connect[a : a + 1, :]
        high = index >> 7
        low = hot(iota((128, count), 0) == index - (high << 7))
        low_ref[a] = low
        mask = high_hot(high)
        highs.append(mask)
        got = dot(table, low)
        picked.append(jnp.concatenate([jnp.where(mask, got[8 * i : 8 * i + 8], 0.0) for i in range(6)], axis=0).astype(BF16))
    spread = hot(iota((24, 384), 1) // 16 == iota((24, 384), 0))
    m_high, m_low = split(matrix)
    wide = jnp.concatenate([dot(m_high, spread), dot(m_low, spread)], axis=0).astype(BF16)
    force = dot(wide, jnp.concatenate(picked, axis=0))
    force = (force[:24] + force[24:]) * stiffness
    total = jnp.zeros((48, 128), F32)
    for a in range(8):
        parts = []
        for c in range(3):
            for part in split(force[3 * a + c : 3 * a + c + 1]):
                parts.append(jnp.where(highs[a], part.astype(F32), 0.0))
        total = total + dot_nt(jnp.concatenate(parts, axis=0).astype(BF16), low_ref[a])
    total_ref[...] = total


def scatter_faces(nodal, low_rows, high_rows, total):
    count = nodal.shape[1]
    for a in range(4):
        low = hot(iota((128, count), 0) == low_rows[a : a + 1])
        mask = high_hot(high_rows[a : a + 1])
        parts = []
        for c in range(3):
            for part in split(nodal[3 * a + c : 3 * a + c + 1]):
                parts.append(jnp.where(mask, part.astype(F32), 0.0))
        total = total - dot_nt(jnp.concatenate(parts, axis=0).astype(BF16), low)
    return total


def segment_masks(segment):
    half = (iota(segment.shape, 1) >= 64).astype(F32)
    return [segment - half == 2.0 * p for p in range(4)]


def contact(meta_ref, blocks_ref, sorted_ref, segment_ref, gap_ref, force_ref):
    steps = (meta_ref[2, 0] + (GROUP - 1)) // GROUP

    def gap_step(i, _):
        for k in range(GROUP):
            t = i * GROUP + k
            owner, start = meta_ref[0, t], meta_ref[1, t]
            disp = sorted_ref[pl.ds(start, TILE), :].astype(BF16)[:, 0:64]
            masks = segment_masks(segment_ref[pl.ds(start, TILE), :])
            every = dot(disp, blocks_ref[owner, 0:64, :])
            offset = blocks_ref[owner, 64:72, :].astype(F32)[0:1]
            gap = jnp.zeros((TILE, 128), F32)
            for p in range(4):
                at = slice(128 * p, 128 * p + 128)
                gap = jnp.where(masks[p], every[:, at] - offset[:, at], gap)
            gap_ref[pl.ds(start, TILE), :] = gap
        return 0

    lax.fori_loop(0, steps, gap_step, 0)
    gap = gap_ref[0:2048]
    gap_ref[0:2048] = jnp.maximum(-gap, 0.0) + jnp.log(1.0 + jnp.exp(-jnp.abs(gap)))

    def force_step(i, _):
        for k in range(GROUP):
            t = i * GROUP + k
            owner, start = meta_ref[0, t], meta_ref[1, t]
            traction = gap_ref[pl.ds(start, TILE), :]
            masks = segment_masks(segment_ref[pl.ds(start, TILE), :])
            high, low = split(traction)
            high, low = high.astype(F32), low.astype(F32)
            spread = jnp.concatenate(
                [jnp.concatenate([jnp.where(m, part, 0.0) for m in masks], axis=1) for part in (high, low)], axis=0
            ).astype(BF16)
            force = dot_nt(spread, blocks_ref[owner, 0:64, :])
            force = force[:TILE] + force[TILE:]
            force_ref[pl.ds(start, TILE), :] = jnp.concatenate([force, jnp.zeros_like(force)], axis=1)
        return 0

    lax.fori_loop(0, steps, force_step, 0)


NX, NZ = 4, 8
MESH = pl.DeviceIdType.MESH
BLOCK = 72
A, B = (0, 32), (32, 40)
A0, A1, B0, B1 = (0, 16), (16, 16), (32, 24), (56, 16)


def sign(d):
    return "+" if d > 0 else "-"


def transfers():
    t = []

    def add(*entry):
        t.append(entry)

    for d in (1, -1):
        add("aX" + sign(d), ("x", d), 0, 0, A, ())
        add("aZ1_0" + sign(d), ("z", d), 0, 0, A, ())
        add("bZ1" + sign(d), ("z", d), 0, 0, B, ())
        add("bX0" + sign(d), ("x", d), 0, 0, B, ())
    add("so", ("s", 1), 0, 0, B, ())
    add("aX2+", ("x", 1), -1, 0, A0, ("aX+",))
    add("aX2-", ("x", -1), 1, 0, A1, ("aX-",))
    src = {0: (), -1: ("aX+",), 1: ("aX-",), 2: ("aX2+", "aX2-")}
    for d in (1, -1):
        q = sign(d)
        for rx in (-1, 1, 2):
            add(f"aZ1_{rx}" + q, ("z", d), rx, 0, A, src[rx])
        for k in (2, 3):
            for rx in (0, -1, 1, 2):
                add(f"aZ{k}_{rx}" + q, ("z", d), rx, -(k - 1) * d, A, (f"aZ{k - 1}_{rx}" + q,))
        for rx in (0, 2) if d > 0 else (-1, 1):
            add(f"aZ4_{rx}" + q, ("z", d), rx, -3 * d, A, (f"aZ3_{rx}" + q,))
        add("bZ2" + q, ("z", d), 0, -d, B, ("bZ1" + q,))
        add("bZ3" + q, ("z", d), 0, -2 * d, B, ("bZ2" + q,))
        add("bZ4" + q, ("z", d), 0, -3 * d, B0 if d > 0 else B1, ("bZ3" + q,))
    came = {0: (), -1: ("bZ1+",), 1: ("bZ1-",), -2: ("bZ2+",), 2: ("bZ2-",), -3: ("bZ3+",), 3: ("bZ3-",), 4: ("bZ4+", "bZ4-")}
    for rz in (-1, 1, -2, 2, -3, 3, 4):
        for d in (1, -1):
            add(f"bX{rz}" + sign(d), ("x", d), 0, rz, B, came[rz])
    for rz in (0, -1, 1, -2, 2, -3, 3, 4):
        d = 1 if rz in (0, 1, 2, 3) else -1
        add(f"bY{rz}", ("x", d), -d, rz, B, (f"bX{rz}" + sign(d),))
    add("s_x", ("s", 1), None, 0, A, ("aX+", "aX-", "aX2+", "aX2-"))
    for d in (1, -1):
        q = sign(d)
        for k in (1, 2, 3):
            add(f"sz{k}" + q, ("s", 1), None, -k * d, A, tuple(f"aZ{k}_{rx}" + q for rx in (0, -1, 1, 2)))
    add("sz4", ("s", 1), None, 4, A, ("aZ4_0+", "aZ4_2+", "aZ4_-1-", "aZ4_1-"))
    for rz in (-1, 1, -2, 2, -3, 3, 4):
        add(f"sb{rz}", ("s", 1), 0, rz, B, came[rz])
    for rz in (0, -1, 1, -2, 2, -3, 3, 4):
        add(f"sx{rz}p", ("s", 1), -1, rz, B, (f"bX{rz}+",))
        add(f"sx{rz}m", ("s", 1), 1, rz, B, (f"bX{rz}-",))
        add(f"sx{rz}f", ("s", 1), 2, rz, B, (f"bY{rz}",))
    return t


COPIES = len(transfers())
ORDER = [0, 1, 2, 3, 4, 5, 6, 7, 8, -1, 9, 11, 27, -5, 10, 12, 28, -4, 57, 80, -2, 14, -8, 81, -6, 30, -10, -3, 24, 43, 44, 73, -7, 40, 45, 46, 74, -11, 13, 29, 65, -58, 82, -12, 15, -28, 31, -13, 16, -29, 32, -15, 18, -45, 58, 84, -44, 83, -31, 34, -47, 87, -25, 25, 47, 48, 75, -46, 59, 86, -41, 41, 49, 50, 76, -14, 17, 66, -30, 33, 69, -16, 19, -59, 85, -32, 35, -48, 89, -17, 20, -33, 36, -49, 60, 90, -19, 22, -35, -60, 88, -51, 93, -26, 26, 51, 52, 77, -50, 61, 92, -42, 42, 53, 54, 78, -18, 21, 67, -34, 37, 70, -20, -61, 91, -36, 38, -23, -52, 95, -53, 62, 96, -21, -37, 39, -62, 94, -27, -43, 55, 56, 79, -55, 99, -54, 63, 98, -22, 23, 68, -38, 71, -63, 97, -39, -57, 64, 102, -40, -56, 101, -64, 100, -24, 72, -65, 103, -9, -81, -82, -74, -75, -66, -83, -85, -84, -76, -88, -87, -77, -67, -70, -90, -86, -91, -89, -94, -78, -93, -79, -68, -71, -92, -96, -97, -95, -100, -80, -99, -69, -98, -72, -101, -103, -102, -73, -104]


class Gather:
    def __init__(self, mine, blocks, send_sem, recv_sem):
        self.mine, self.blocks, self.send_sem, self.recv_sem = mine, blocks, send_sem, recv_sem
        v, self.y = lax.axis_index("vol"), lax.axis_index("slab")
        self.v, self.x, self.z, self.c = v, v // 16, (v // 2) % NZ, v % 2
        self.table = transfers()

    def device(self, direction):
        kind, d = direction
        if kind == "x":
            return (((self.x + d + NX) % NX * NZ + self.z) * 2 + self.c, self.y)
        if kind == "z":
            return ((self.x * NZ + (self.z + d + NZ) % NZ) * 2 + self.c, self.y)
        return (self.v + 1 - 2 * self.c, self.y)

    def at(self, rx, rz, core, rows):
        xs = slice(None) if rx is None else (self.x + rx + NX) % NX
        return self.blocks.at[xs, (self.z + rz + NZ) % NZ, core, pl.ds(*rows)]

    def copy(self, i, arriving=False):
        _, direction, rx, rz, rows, after = self.table[i]
        kind, d = direction
        if arriving:
            rx = rx - d if kind == "x" else rx
            rz = rz - d if kind == "z" else rz
            source = target = self.at(rx, rz, 1 - self.c if kind == "s" else self.c, rows)
        else:
            target = self.at(rx, rz, self.c, rows)
            source = target if after else self.mine.at[pl.ds(*rows)]
        return pltpu.make_async_remote_copy(
            src_ref=source, dst_ref=target, send_sem=self.send_sem.at[i], recv_sem=self.recv_sem.at[i],
            device_id=self.device(direction), device_id_type=MESH)

    def greet(self):
        barrier = pltpu.get_barrier_semaphore()
        for direction in (("x", 1), ("x", -1), ("z", 1), ("z", -1), ("s", 1)):
            pl.semaphore_signal(barrier, inc=1, device_id=self.device(direction), device_id_type=MESH)
        return lambda: pl.semaphore_wait(barrier, 5)

    def run(self, events):
        for e in events:
            if e >= 0:
                self.copy(e).start()
            else:
                self.copy(~e, True).wait_recv()

    def leave(self):
        for i in range(COPIES):
            self.copy(i).wait_send()


ANY = pl.BlockSpec(memory_space=pl.ANY)
VM = pl.BlockSpec(memory_space=pltpu.VMEM)
SM = pl.BlockSpec(memory_space=pltpu.SMEM)


def kernel_a(*refs):
    inputs, outputs, buffers = refs[:11], refs[11:15], refs[15:26]
    mine, low_ref, load_sem, own_sem, send_sem, recv_sem = refs[26:]
    blocks_ref, sorted_ref, meta_ref, total_ref = outputs
    gather = Gather(mine, blocks_ref, send_sem, recv_sem)
    enter = gather.greet()
    loads = [pltpu.make_async_copy(s, d, load_sem.at[k]) for k, (s, d) in enumerate(zip(inputs, buffers))]
    for load in loads:
        load.start()
    mortar, offset, owner, disp, segment, area, nodes, node, stiffness, connect, matrix = buffers
    loads[0].wait()
    loads[1].wait()
    eye = hot(iota((64, 64), 0) == iota((64, 64), 1))
    mine[0:64, :] = dot_nt(eye, mortar[...].reshape(512, 64)).astype(BF16)
    gaps = offset[...].astype(F32)
    line = jnp.concatenate([gaps[g : g + 1] for g in range(8)], axis=1)
    mine[64:72, :] = jnp.broadcast_to(line, (8, 512)).astype(BF16)
    own = pltpu.make_async_copy(mine, gather.at(0, 0, gather.c, (0, BLOCK)), own_sem)
    own.start()
    enter()
    own.wait()
    gather.run(ORDER[:9])
    for load in loads[2:]:
        load.wait()
    row, count, first, before = sort_faces(owner[...], 64)
    meta_ref[...] = tile_table(count, first, before)
    permute(row, disp[...], segment[...], area[...], nodes[...], sorted_ref)
    elements(node[...], connect[...], stiffness[...], matrix[...], total_ref, low_ref)
    gather.run(ORDER[9:])
    gather.leave()


def stage_a(*arrays):
    return pl.pallas_call(
        kernel_a,
        out_shape=(
            jax.ShapeDtypeStruct((NX, NZ, 2, BLOCK, 512), BF16),
            jax.ShapeDtypeStruct((2048, 256), F32),
            jax.ShapeDtypeStruct((8, 128), I32),
            jax.ShapeDtypeStruct((48, 128), F32),
        ),
        in_specs=[ANY] * 11,
        out_specs=(ANY, VM, VM, VM),
        scratch_shapes=[pltpu.VMEM(a.shape, a.dtype) for a in arrays]
        + [
            pltpu.VMEM((BLOCK, 512), BF16),
            pltpu.VMEM((8, 128, 1024), BF16),
            pltpu.SemaphoreType.DMA((11,)),
            pltpu.SemaphoreType.DMA,
            pltpu.SemaphoreType.DMA((COPIES,)),
            pltpu.SemaphoreType.DMA((COPIES,)),
        ],
        compiler_params=pltpu.CompilerParams(collective_id=0, has_side_effects=True, vmem_limit_bytes=60 << 20),
        name="gather_blocks",
    )(*arrays)


def kernel_b(meta_ref, blocks_in, sorted_in, force_ref, blocks_ref, sorted_ref, segment_ref, gap_ref, out_ref, sem):
    load = pltpu.make_async_copy(blocks_in, blocks_ref, sem)
    load.start()
    sorted_ref[0:2048, :] = sorted_in[:, 0:128]
    segment_ref[0:2048, :] = sorted_in[:, 128:256]
    sorted_ref[2048:, :] = jnp.zeros((TILE, 128), F32)
    segment_ref[2048:, :] = jnp.zeros((TILE, 128), F32)
    load.wait()
    contact(meta_ref, blocks_ref, sorted_ref, segment_ref, gap_ref, out_ref)
    force_ref[...] = out_ref[0:2048, :].astype(BF16)


def stage_b(meta, blocks, rows):
    return pl.pallas_call(
        kernel_b,
        out_shape=jax.ShapeDtypeStruct((2048, 128), BF16),
        in_specs=[SM, ANY, VM],
        out_specs=VM,
        scratch_shapes=[
            pltpu.VMEM((64, BLOCK, 512), BF16),
            pltpu.VMEM((2048 + TILE, 128), F32),
            pltpu.VMEM((2048 + TILE, 128), F32),
            pltpu.VMEM((2048 + TILE, 128), F32),
            pltpu.VMEM((2048 + TILE, 128), F32),
            pltpu.SemaphoreType.DMA,
        ],
        compiler_params=pltpu.CompilerParams(vmem_limit_bytes=48 << 20),
        name="contact_tiles",
    )(meta, blocks.reshape(64, BLOCK, 512), rows)


def finish(rows, force, shape, total):
    choose = hot(iota((16, 128), 1) == iota((16, 128), 0) + 64)
    extra = dot_nt(choose, rows)
    area = extra[8:9] + extra[9:10] + extra[10:11]
    s_high, s_low = split(shape)
    nodal = dot_nt(jnp.concatenate([s_high.astype(F32), s_low.astype(F32)], axis=0).astype(BF16), force)
    nodal = (nodal[:12] + nodal[12:]) * area
    return scatter_faces(nodal, extra[0:4].astype(I32), extra[4:8].astype(I32), total)


def kernel_c(sorted_ref, force_ref, shape_ref, total_ref, out_ref, rims, came, send_sem, recv_sem):
    v, y = lax.axis_index("vol"), lax.axis_index("slab")
    slabs = lax.axis_size("slab")
    up, down = (v, (y + 1) % slabs), (v, (y + slabs - 1) % slabs)
    barrier = pltpu.get_barrier_semaphore()
    for peer in (up, down):
        pl.semaphore_signal(barrier, inc=1, device_id=peer, device_id_type=MESH)
    total = finish(sorted_ref[:, 0:128].astype(BF16), force_ref[:, 0:64], shape_ref[...], total_ref[...])
    grids = [total[16 * c : 16 * c + 8] + total[16 * c + 8 : 16 * c + 16] for c in range(3)]
    for c in range(3):
        rims[8 * c : 8 * c + 8] = grids[c]
    pl.semaphore_wait(barrier, 2)
    copies = [
        pltpu.make_async_remote_copy(
            src_ref=rims, dst_ref=came.at[k], send_sem=send_sem.at[k], recv_sem=recv_sem.at[k], device_id=peer, device_id_type=MESH)
        for k, peer in enumerate((up, down))
    ]
    for copy in copies:
        copy.start()
    for copy in copies:
        copy.wait()
    for c in range(3):
        for h in range(8):
            line = grids[c][h : h + 1]
            if h < 2:
                line = line + jnp.where(y > 0, came[0, 8 * c + h + 6 : 8 * c + h + 7], 0.0)
            if h >= 6:
                line = line + jnp.where(y < slabs - 1, came[1, 8 * c + h - 6 : 8 * c + h - 5], 0.0)
            out_ref[c : c + 1, 128 * h : 128 * h + 128] = line


def stage_c(rows, force, shape, total):
    return pl.pallas_call(
        kernel_c,
        out_shape=jax.ShapeDtypeStruct((3, 1024), F32),
        in_specs=[VM] * 4,
        out_specs=VM,
        scratch_shapes=[
            pltpu.VMEM((24, 128), F32),
            pltpu.VMEM((2, 24, 128), F32),
            pltpu.SemaphoreType.DMA((2,)),
            pltpu.SemaphoreType.DMA((2,)),
        ],
        compiler_params=pltpu.CompilerParams(collective_id=1, has_side_effects=True, vmem_limit_bytes=32 << 20),
        name="faces_and_rims",
    )(rows, force, shape, total)


def shards(face_disp, contact_owner, segment, face_area, face_nodes, mortar_blocks, gap_offset, shape_table, node_disp, stiffness, connect, elem_matrix):
    blocks, rows, meta, total = stage_a(
        mortar_blocks, gap_offset, contact_owner.reshape(1, 2048), face_disp, segment.reshape(1, 2048),
        face_area.reshape(1, 2048), face_nodes, node_disp, stiffness.reshape(1, 1024), connect, elem_matrix)
    force = stage_b(meta, blocks, rows)
    return stage_c(rows, force, shape_table, total)


def solution(mesh):
    both = ("vol", "slab")
    in_specs = (
        P(None, both), P(both, None), P(both), P(both), P(None, both), P(both, None, None), P(both, None), P(),
        P(None, both), P(both), P(None, both), P())
    return jax.shard_map(shards, mesh=mesh, in_specs=in_specs, out_specs=P(None, both), check_vma=False)
```

profile of v0, /device:TPU:1, one launch (start us, length us, event | category | flops | bytes accessed | tf_op | source)
XLA Modules:
  0.0 63.6 jit_solution(13273926105099945824)
XLA Ops:
  0.0 0.0 copy-start.2
  0.0 42.8 %gather_blocks.1 = (bf16[4,8,2,72,512]{4,3,2,1,0:T(8,128)(2,1)}, f32[2048,256]{1,0:T(8,128)}, s32[8,128]{1,0:T(8,128)}, f32[48,128]{1,0:T(8,128)}) custom-call(bf16[8,64,64]{2,1,0:T(8,128)(2,1)} %refs_0_.1, bf16[8,64]{1,0:T(8,128)(2,1)} %refs_1_.1, s32[1,2048]{1,0:T(1,128)} %bitcast.6, bf16[64,2048]{1,0:T(8,128)(2,1)} %refs_3_.1, s32[1,2048]{1,0:T(1,128)} %bitcast.7, ...), custom_call_target="tpu_custom_call" | custom-call | tf_op jit(solution)/shard_map/gather_blocks/pallas_call | solution.py:345
  42.8 0.0 copy-start
  42.8 1.6 %copy-done = f32[2048,256]{1,0:T(8,128)S(1)} copy-done((f32[2048,256]{1,0:T(8,128)S(1)}, f32[2048,256]{1,0:T(8,128)}, u32[]{:S(2)}) %copy-start) | copy-done | bytes 2097176
  44.4 0.0 copy-start.3
  44.4 0.7 %copy-done.3 = s32[8,128]{1,0:T(8,128)S(1)} copy-done((s32[8,128]{1,0:T(8,128)S(1)}, s32[8,128]{1,0:T(8,128)}, u32[]{:S(2)}) %copy-start.3) | copy-done | bytes 4120
  45.1 0.0 copy-start.1
  45.1 12.7 %contact_tiles.1.force_ref = bf16[2048,128]{1,0:T(8,128)(2,1)S(1)} custom-call(s32[8,128]{1,0:T(8,128)S(1)} %copy-done.3, bf16[64,72,512]{2,1,0:T(8,128)(2,1)} %bitcast.5, f32[2048,256]{1,0:T(8,128)S(1)} %copy-done), custom_call_target="tpu_custom_call" | custom-call | tf_op jit(solution)/shard_map/contact_tiles/pallas_call | solution.py:382
  57.8 0.0 copy-done.2
  57.8 0.0 copy-done.1
  57.8 5.2 %faces_and_rims.1 = f32[3,1024]{1,0:T(4,128)S(1)} custom-call(f32[2048,256]{1,0:T(8,128)S(1)} %copy-done, bf16[2048,128]{1,0:T(8,128)(2,1)S(1)} %contact_tiles.1.force_ref, f32[12,64]{1,0:T(8,128)S(1)} %copy-done.2, f32[48,128]{1,0:T(8,128)S(1)} %copy-done.1), custom_call_target="tpu_custom_call" | custom-call | tf_op jit(solution)/shard_map/faces_and_rims/pallas_call | solution.py:442
  63.0 0.6 copy.14
Async XLA Ops:
  0.0 57.8 %copy-start.2 = (f32[12,64]{1,0:T(8,128)S(1)}, f32[12,64]{1,0:T(8,128)}, u32[]{:S(2)}) copy-start(f32[12,64]{1,0:T(8,128)} %shape_ref.1) | copy-start | bytes 9220
  42.8 1.6 %copy-start = (f32[2048,256]{1,0:T(8,128)S(1)}, f32[2048,256]{1,0:T(8,128)}, u32[]{:S(2)}) copy-start(f32[2048,256]{1,0:T(8,128)} %get-tuple-element.9.sorted_in.sorted_ref) | copy-start | bytes 6291460
  44.4 0.7 %copy-start.3 = (s32[8,128]{1,0:T(8,128)S(1)}, s32[8,128]{1,0:T(8,128)}, u32[]{:S(2)}) copy-start(s32[8,128]{1,0:T(8,128)} %get-tuple-element.10.meta_ref) | copy-start | bytes 12292
  45.1 12.8 %copy-start.1 = (f32[48,128]{1,0:T(8,128)S(1)}, f32[48,128]{1,0:T(8,128)}, u32[]{:S(2)}) copy-start(f32[48,128]{1,0:T(8,128)} %get-tuple-element.12.total_ref) | copy-start | bytes 73732
where the time goes:
time: 63.8 us; the launch traced here: 63.6 us
  Pallas kernels  60.7 us (95%)
  local copies, waits for them, and re-layouts  2.87 us (4%)
    pallas_call x1, Pallas kernels, stage_a(): pl.pallas_call(kernel_a, out_shape=(jax.ShapeDtypeStruct((NX, NZ, 2, BLOC...  42.8 us
    pallas_call x1, Pallas kernels, stage_b(): pl.pallas_call(kernel_b, out_shape=jax.ShapeDtypeStruct((2048, 128), BF16...  12.7 us
    pallas_call x1, Pallas kernels, stage_c(): pl.pallas_call(kernel_c, out_shape=jax.ShapeDtypeStruct((3, 1024), F32),...  5.18 us
    unnamed x9, local copies, waits for them, and re-layouts  2.87 us

commit v1 on v0

v1 whole, which is shorter than its diff:
```python
import functools

import jax
import jax.numpy as jnp
from jax import lax
from jax.experimental import pallas as pl
from jax.experimental.pallas import tpu as pltpu
from jax.sharding import PartitionSpec as P

SH = 256
TILE = 32
CAP = 128
F32, BF16, I32 = jnp.float32, jnp.bfloat16, jnp.int32
NT = (((1,), (1,)), ((), ()))


def dot(a, b):
    return jnp.dot(a, b, preferred_element_type=F32)


def dot_nt(a, b):
    return lax.dot_general(a, b, NT, preferred_element_type=F32)


def iota(shape, dim):
    return lax.broadcasted_iota(I32, shape, dim)


def hot(mask):
    return jnp.where(mask, 1.0, 0.0).astype(BF16)


def split(value):
    high = value.astype(BF16)
    return high, (value - high.astype(F32)).astype(BF16)


def sort_faces(owner, owners):
    faces = owner.shape[1]
    member = iota((owners, faces), 0) == owner
    member_low = hot(member)
    upto = hot(iota((256, 256), 0) <= iota((256, 256), 1))
    carry = jnp.zeros((owners, 1), F32)
    parts = []
    for k in range(faces // 256):
        part = dot(member_low[:, 256 * k : 256 * k + 256], upto) + carry
        carry = part[:, 255:256]
        parts.append(part)
    rank = jnp.concatenate(parts, axis=1)
    before = hot(iota((owners, owners), 1) < iota((owners, owners), 0))
    count = jnp.broadcast_to(carry, (owners, 128))
    first = dot(before, count.astype(BF16))
    row = jnp.sum(jnp.where(member, rank - 1.0 + first[:, 0:1], 0.0), axis=0, keepdims=True)
    return row.astype(I32), count, first


def owner_table(first, count):
    owners = first.shape[0]
    mine = iota((owners, 128), 0) == iota((owners, 128), 1)
    lines = [jnp.sum(jnp.where(mine, value, 0.0), axis=0, keepdims=True) for value in (first, count)]
    return jnp.concatenate(lines + [jnp.zeros((6, 128), F32)], axis=0).astype(I32)


def face_content(disp, segment, area, nodes):
    faces = disp.shape[1]
    nodes_high = nodes >> 7
    area_a = area.astype(BF16)
    area_b, area_c = split(area - area_a.astype(F32))
    extra = jnp.concatenate([(nodes - (nodes_high << 7)).astype(F32), nodes_high.astype(F32)], axis=0).astype(BF16)
    return [
        disp,
        extra,
        area_a,
        area_b,
        area_c,
        jnp.zeros((53, faces), BF16),
        jnp.broadcast_to(segment.astype(F32), (128, faces)).astype(BF16),
    ]


def permute_rows(k, row, content, sorted_ref, segment_ref):
    pick = hot(iota((256, row.shape[1]), 0) + 256 * k == row)
    part = dot_nt(pick, content)
    sorted_ref[256 * k : 256 * k + 256, :] = part[:, 0:128]
    segment_ref[256 * k : 256 * k + 256, :] = part[:, 128:256] - (iota((256, 128), 1) >= 64).astype(F32)


def high_hot(high_row):
    return iota((8, high_row.shape[1]), 0) == high_row


def elements(node, connect, stiffness, matrix, total_ref, low_ref):
    count = connect.shape[1]
    rows = []
    for c in range(3):
        grid = jnp.concatenate([node[c : c + 1, 128 * h : 128 * h + 128] for h in range(8)], axis=0)
        high, low = split(grid)
        rows += [high.astype(F32), low.astype(F32)]
    table = jnp.concatenate(rows, axis=0).astype(BF16)
    picked, highs = [], []
    for a in range(8):
        index = connect[a : a + 1, :]
        high = index >> 7
        low = hot(iota((128, count), 0) == index - (high << 7))
        low_ref[a] = low
        mask = high_hot(high)
        highs.append(mask)
        got = dot(table, low)
        picked.append(jnp.concatenate([jnp.where(mask, got[8 * i : 8 * i + 8], 0.0) for i in range(6)], axis=0).astype(BF16))
    spread = hot(iota((24, 384), 1) // 16 == iota((24, 384), 0))
    m_high, m_low = split(matrix)
    wide = jnp.concatenate([dot(m_high, spread), dot(m_low, spread)], axis=0).astype(BF16)
    force = dot(wide, jnp.concatenate(picked, axis=0))
    force = (force[:24] + force[24:]) * stiffness
    total = jnp.zeros((48, 128), F32)
    for a in range(8):
        parts = []
        for c in range(3):
            for part in split(force[3 * a + c : 3 * a + c + 1]):
                parts.append(jnp.where(highs[a], part.astype(F32), 0.0))
        total = total + dot_nt(jnp.concatenate(parts, axis=0).astype(BF16), low_ref[a])
    total_ref[...] += total


def scatter_faces(nodal, low_rows, high_rows, total):
    count = nodal.shape[1]
    for a in range(4):
        low = hot(iota((128, count), 0) == low_rows[a : a + 1])
        mask = high_hot(high_rows[a : a + 1])
        parts = []
        for c in range(3):
            for part in split(nodal[3 * a + c : 3 * a + c + 1]):
                parts.append(jnp.where(mask, part.astype(F32), 0.0))
        total = total - dot_nt(jnp.concatenate(parts, axis=0).astype(BF16), low)
    return total


def segment_masks(segment):
    return [segment == 2.0 * p for p in range(4)]


NX, NZ = 4, 8
MESH = pl.DeviceIdType.MESH
BLOCK = 72
A, B = (0, 16), (16, 56)
B0, B1 = (16, 24), (40, 32)
RING = (0, -1, 1, -2, 2, -3, 3, 4)


def sign(d):
    return "+" if d > 0 else "-"


def transfers():
    t = []

    def add(*entry):
        t.append(entry)

    for d in (1, -1):
        add("z1" + sign(d), ("z", d), ("one", 0, 0), B, ())
        add("z2" + sign(d), ("z", 2 * d), ("one", 0, 0), B, ())
    for d in (1, -1):
        add("ax" + sign(d), ("x", d), ("one", 0, 0), A, ())
    add("a2", ("x", 2), ("one", 0, 0), A, ())
    for d in (1, -1):
        add("z3" + sign(d), ("z", 2 * d), ("one", 0, -d), B, ("z1" + sign(d),))
        add("z4" + sign(d), ("z", 2 * d), ("one", 0, -2 * d), B0 if d > 0 else B1, ("z2" + sign(d),))
    a_line = ("ax+", "ax-", "a2")
    for d in (1, -1):
        add("az1" + sign(d), ("z", d), ("x_all", 0, 0), A, a_line)
        add("az2" + sign(d), ("z", 2 * d), ("x_all", 0, 0), A, a_line)
    for k in RING:
        for d in (1, -1):
            add(f"x{k}" + sign(d), ("x", d), ("one", 0, k), B, z_arrivals(k))
    for d in (1, -1):
        add("az3" + sign(d), ("z", 2 * d), ("x_all", 0, -d), A, ("az1" + sign(d),))
        add("az4" + sign(d), ("z", 2 * d), ("x_low" if d > 0 else "x_high", 0, -2 * d), A, ("az2" + sign(d),))
    for k in RING:
        d = 1 if k in (0, 1, 2, 3) else -1
        add(f"y{k}", ("x", d), ("one", -d, k), B, (f"x{k}" + sign(d),))
    add("s0", ("s", 1), ("z_all", 0, 0), B, tuple(q for k in RING for q in z_arrivals(k)))
    add("s-1", ("s", 1), ("z_all", -1, 0), B, tuple(f"x{k}+" for k in RING))
    add("s1", ("s", 1), ("z_all", 1, 0), B, tuple(f"x{k}-" for k in RING))
    add("sa", ("s", 1), ("all", 0, 0), A, a_line + tuple(q for k in RING for q in az_arrivals(k)))
    for k in RING:
        add(f"sy{k}", ("s", 1), ("one", 2, k), B, (f"y{k}",))
    return t


def z_arrivals(k):
    if k == 0:
        return ()
    if k == 4:
        return ("z4+", "z4-")
    return (f"z{abs(k)}" + sign(-k),)


def az_arrivals(k):
    return tuple("a" + q for q in z_arrivals(k))


def needed(core, rx, k):
    if core:
        return {"sa"} | ({f"sy{k}"} if rx == 2 else {f"s{rx}"})
    part_a = set(az_arrivals(k)) if k else set({0: (), -1: ("ax+",), 1: ("ax-",), 2: ("a2",)}[rx])
    part_b = set(z_arrivals(k)) if rx == 0 else {{-1: f"x{k}+", 1: f"x{k}-", 2: f"y{k}"}[rx]}
    return part_a | part_b


EXPECTED = {
    "z1": 6.0, "z2": 7.0, "ax": 6.2, "a2": 6.6, "x0": 8.0, "z3": 10.0, "z4": 11.0, "az1": 10.2, "az2": 11.2, "x-1": 9.0, "x1": 9.0,
    "x-2": 12.0, "x2": 12.0, "az3": 14.0, "az4": 15.0, "x-3": 15.0, "x3": 15.0, "x4": 16.0, "y0": 12.5, "y-1": 14.5, "y1": 14.5,
    "y-2": 17.0, "y2": 17.0, "y-3": 20.0, "y3": 20.0, "y4": 21.0, "s0": 13.0, "sa": 16.5, "s-1": 18.0, "s1": 18.0,
}


def expected(name):
    if name.startswith("sy"):
        return EXPECTED[name[1:]] + 2.0
    return EXPECTED[name.rstrip("+-") if name not in EXPECTED else name]


def event_order(table):
    started, seen, order = set(), set(), []

    def start():
        ready = [i for i, entry in enumerate(table) if i not in started and all(q in seen for q in entry[4])]
        for i in sorted(ready, key=lambda i: (table[i][1][0] == "s", i)):
            order.append(i)
            started.add(i)

    start()
    for i in sorted(range(len(table)), key=lambda i: (expected(table[i][0]), i)):
        order.append(~i)
        seen.add(table[i][0])
        start()
    return order


COPIES = len(transfers())


class Gather:
    def __init__(self, mine, blocks, send_sem, recv_sem):
        self.mine, self.blocks, self.send_sem, self.recv_sem = mine, blocks, send_sem, recv_sem
        v, self.y = lax.axis_index("vol"), lax.axis_index("slab")
        self.x, self.z, self.c = v // (2 * NZ), (v // 2) % NZ, v % 2
        self.table = transfers()
        self.order = event_order(self.table)

    def place(self, direction, way=1):
        kind, d = direction
        if kind == "x":
            return (self.x + way * d + NX) % NX, self.z, self.c
        if kind == "z":
            return self.x, (self.z + way * d + NZ) % NZ, self.c
        return self.x, self.z, 1 - self.c

    def device(self, direction, way=1):
        x, z, c = self.place(direction, way)
        return ((x * NZ + z) * 2 + c, self.y)

    def at(self, spec, x, z, core, rows):
        kind, rx, rz = spec
        x, z, r = (x + rx + NX) % NX, (z + rz + NZ) % NZ, pl.ds(*rows)
        if kind == "x_all":
            return self.blocks.at[:, z, core, r]
        if kind == "x_low":
            return self.blocks.at[pl.ds(0, 2), z, core, r]
        if kind == "x_high":
            return self.blocks.at[pl.ds(2, 2), z, core, r]
        if kind == "z_all":
            return self.blocks.at[x, :, core, r]
        if kind == "all":
            return self.blocks.at[:, :, core, r]
        return self.blocks.at[x, z, core, r]

    def copy(self, i, arriving=False):
        _, direction, spec, rows, after = self.table[i]
        if arriving:
            source = target = self.at(spec, *self.place(direction, -1), rows)
        else:
            target = self.at(spec, self.x, self.z, self.c, rows)
            source = target if after else self.mine.at[pl.ds(*rows)]
        return pltpu.make_async_remote_copy(
            src_ref=source, dst_ref=target, send_sem=self.send_sem.at[i], recv_sem=self.recv_sem.at[i],
            device_id=self.device(direction), device_id_type=MESH)

    def greet(self, others):
        barrier = pltpu.get_barrier_semaphore()
        directions = list(dict.fromkeys(entry[1] for entry in self.table))
        for direction in directions:
            pl.semaphore_signal(barrier, inc=1, device_id=self.device(direction, -1), device_id_type=MESH)
        for peer in others:
            pl.semaphore_signal(barrier, inc=1, device_id=peer, device_id_type=MESH)
        return lambda: pl.semaphore_wait(barrier, len(directions) + len(others))

    def leave(self):
        for i in range(COPIES):
            self.copy(i).wait_send()


ANY = pl.BlockSpec(memory_space=pl.ANY)
VM = pl.BlockSpec(memory_space=pltpu.VMEM)


def owner_force(x, z, core, table, blocks_ref, sorted_ref, segment_ref):
    owner = (x * NZ + z) * 2 + core
    first = jnp.clip(table[0, owner], 0, sorted_ref.shape[0] - CAP)
    offset = blocks_ref[x, z, core, 64:72, :].astype(F32)[0:1]
    rows = sorted_ref[pl.ds(first, CAP), :].astype(BF16)
    masks = segment_masks(segment_ref[pl.ds(first, CAP), :])
    every = dot(rows[:, 0:64], blocks_ref[x, z, core, 0:64, :])
    gap = jnp.zeros((CAP, 128), F32)
    for p in range(4):
        at = slice(128 * p, 128 * p + 128)
        gap = jnp.where(masks[p], every[:, at] - offset[:, at], gap)
    traction = jnp.maximum(-gap, 0.0) + jnp.log(1.0 + jnp.exp(-jnp.abs(gap)))
    parts = [jnp.concatenate([jnp.where(m, part.astype(F32), 0.0) for m in masks], axis=1) for part in split(traction)]
    force = dot_nt(jnp.concatenate(parts, axis=0).astype(BF16), blocks_ref[x, z, core, 0:64, :])
    held = jnp.where(iota((1, CAP), 1) < table[1, owner], 1.0, 0.0)
    return rows, (force[:CAP] + force[CAP:]).astype(BF16), held


def spread_faces(found, shape_ref, total_ref):
    rows, force, held = (jnp.concatenate(part, axis=axis) for part, axis in zip(zip(*found), (0, 0, 1)))
    choose = hot(iota((16, 128), 1) == iota((16, 128), 0) + 64)
    extra = dot_nt(choose, rows)
    area = (extra[8:9] + extra[9:10] + extra[10:11]) * held
    s_high, s_low = split(shape_ref[...])
    nodal = dot_nt(jnp.concatenate([s_high.astype(F32), s_low.astype(F32)], axis=0).astype(BF16), force)
    nodal = (nodal[:12] + nodal[12:]) * area
    total_ref[...] = scatter_faces(nodal, extra[0:4].astype(I32), extra[4:8].astype(I32), total_ref[...])


def kernel(*refs):
    inputs, out_ref, buffers = refs[:12], refs[12], refs[13:25]
    blocks_ref, sorted_ref, segment_ref, mine, low_ref, total_ref, table_ref, rims, came, table = refs[25:35]
    load_sem, own_sem, send_sem, recv_sem, rim_send, rim_recv = refs[35:]
    slabs = lax.axis_size("slab")
    gather = Gather(mine, blocks_ref, send_sem, recv_sem)
    v, y = lax.axis_index("vol"), gather.y
    peers = ((v, (y + 1) % slabs), (v, (y + slabs - 1) % slabs))
    enter = gather.greet(peers)
    loads = [pltpu.make_async_copy(s, d, load_sem.at[k]) for k, (s, d) in enumerate(zip(inputs, buffers))]
    for load in loads:
        load.start()
    mortar, offset, owner, disp, segment, area, nodes, node, stiffness, connect, matrix, shape = buffers
    loads[0].wait()
    loads[1].wait()
    eye = hot(iota((64, 64), 0) == iota((64, 64), 1))
    mine[0:64, :] = dot_nt(eye, mortar[...].reshape(512, 64)).astype(BF16)
    gaps = offset[...].astype(F32)
    line = jnp.concatenate([gaps[g : g + 1] for g in range(8)], axis=1)
    mine[64:72, :] = jnp.broadcast_to(line, (8, 512)).astype(BF16)
    own = pltpu.make_async_copy(mine, gather.at(("one", 0, 0), gather.x, gather.z, gather.c, (0, BLOCK)), own_sem.at[0])
    own.start()
    enter()
    first_wait = next(i for i, e in enumerate(gather.order) if e < 0)
    for e in gather.order[:first_wait]:
        gather.copy(e).start()
    for load in loads[2:]:
        load.wait()
    total_ref[...] = jnp.zeros_like(total_ref)
    row, count, first = sort_faces(owner[...], 64)
    table_ref[...] = owner_table(first, count)
    to_smem = pltpu.make_async_copy(table_ref, table, own_sem.at[1])
    to_smem.start()
    content = jnp.concatenate(face_content(disp[...], segment[...], area[...], nodes[...]), axis=0)
    sorted_ref[2048:, :] = jnp.zeros((CAP, 128), F32)
    segment_ref[2048:, :] = jnp.zeros((CAP, 128), F32)
    own.wait()
    to_smem.wait()

    def owners(core, rx, ks):
        found = []
        for k in ks:
            z = (gather.z + k + NZ) % NZ
            x = (gather.x + rx + NX) % NX
            c = 1 - gather.c if core else gather.c
            found.append(owner_force(x, z, c, table, blocks_ref, sorted_ref, segment_ref))
        spread_faces(found, shape, total_ref)

    work = [(set(), lambda k=k: permute_rows(k, row, content, sorted_ref, segment_ref)) for k in range(8)]
    early = {"z1+", "z1-", "z2+", "z2-", "ax+", "ax-", "a2", "x0+", "x0-"}
    late = {"z3+", "z3-", "z4+", "z4-", "az1+", "az1-", "az2+", "az2-"}
    work.append((early, lambda: elements(node[...], connect[...], stiffness[...], matrix[...], total_ref, low_ref)))
    for core in (0, 1):
        for rx in (0, -1, 1, 2):
            for ks in ((0, -1, 1, -2), (2, -3, 3, 4)):
                need = set().union(*[needed(core, rx, k) for k in ks]) | late
                work.append((need, lambda core=core, rx=rx, ks=ks: owners(core, rx, ks)))
    seen = set()

    def do(budget):
        for _ in range(budget):
            for i, (need, piece) in enumerate(work):
                if need <= seen:
                    work.pop(i)
                    piece()
                    break
            else:
                return

    do(BEFORE_FIRST_WAIT)
    for e in gather.order[first_wait:]:
        if e >= 0:
            gather.copy(e).start()
            continue
        gather.copy(~e, True).wait_recv()
        seen.add(gather.table[~e][0])
        do(1)
    do(len(work))
    assert not work
    gather.leave()
    total = total_ref[...]
    grids = [total[16 * c : 16 * c + 8] + total[16 * c + 8 : 16 * c + 16] for c in range(3)]
    for c in range(3):
        rims[8 * c : 8 * c + 8] = grids[c]
    copies = [
        pltpu.make_async_remote_copy(
            src_ref=rims, dst_ref=came.at[k], send_sem=rim_send.at[k], recv_sem=rim_recv.at[k], device_id=peer, device_id_type=MESH)
        for k, peer in enumerate(peers)
    ]
    for copy in copies:
        copy.start()
    for copy in copies:
        copy.wait()
    for c in range(3):
        for h in range(8):
            line = grids[c][h : h + 1]
            if h < 2:
                line = line + jnp.where(y > 0, came[0, 8 * c + h + 6 : 8 * c + h + 7], 0.0)
            if h >= 6:
                line = line + jnp.where(y < slabs - 1, came[1, 8 * c + h - 6 : 8 * c + h - 5], 0.0)
            out_ref[c : c + 1, 128 * h : 128 * h + 128] = line


BEFORE_FIRST_WAIT = 8


def shards(face_disp, contact_owner, segment, face_area, face_nodes, mortar_blocks, gap_offset, shape_table, node_disp, stiffness, connect, elem_matrix):
    arrays = (
        mortar_blocks, gap_offset, contact_owner.reshape(1, 2048), face_disp, segment.reshape(1, 2048),
        face_area.reshape(1, 2048), face_nodes, node_disp, stiffness.reshape(1, 1024), connect, elem_matrix, shape_table)
    return pl.pallas_call(
        kernel,
        out_shape=jax.ShapeDtypeStruct((3, 1024), F32),
        in_specs=[ANY] * 12,
        out_specs=VM,
        scratch_shapes=[pltpu.VMEM(a.shape, a.dtype) for a in arrays]
        + [
            pltpu.VMEM((NX, NZ, 2, BLOCK, 512), BF16),
            pltpu.VMEM((2048 + CAP, 128), F32),
            pltpu.VMEM((2048 + CAP, 128), F32),
            pltpu.VMEM((BLOCK, 512), BF16),
            pltpu.VMEM((8, 128, 1024), BF16),
            pltpu.VMEM((48, 128), F32),
            pltpu.VMEM((8, 128), I32),
            pltpu.VMEM((24, 128), F32),
            pltpu.VMEM((2, 24, 128), F32),
            pltpu.SMEM((8, 128), I32),
            pltpu.SemaphoreType.DMA((12,)),
            pltpu.SemaphoreType.DMA((2,)),
            pltpu.SemaphoreType.DMA((COPIES,)),
            pltpu.SemaphoreType.DMA((COPIES,)),
            pltpu.SemaphoreType.DMA((2,)),
            pltpu.SemaphoreType.DMA((2,)),
        ],
        compiler_params=pltpu.CompilerParams(collective_id=0, has_side_effects=True, vmem_limit_bytes=60 << 20),
        name="contact_residual",
    )(*arrays)


def solution(mesh):
    both = ("vol", "slab")
    in_specs = (
        P(None, both), P(both, None), P(both), P(both), P(None, both), P(both, None, None), P(both, None), P(),
        P(None, both), P(both), P(None, both), P())
    return jax.shard_map(shards, mesh=mesh, in_specs=in_specs, out_specs=P(None, both), check_vma=False)
```

time: 63.8 us -> 51.8 us (0.81)
  Pallas kernels: 60.7 us -> 50.2 us
  local copies, waits for them, and re-layouts: 2.87 us -> 1.33 us
    pallas_call x3 -> x1, Pallas kernels: 60.7 us -> 50.2 us  [shards(): pl.pallas_call(kernel, out_shape=jax.ShapeDtypeStruct((3, 1024), F32), in...]
    unnamed x9 -> x1, local copies, waits for them, and re-layouts: 2.87 us -> 1.33 us
where the time goes in v1:
time: 51.8 us; the launch traced here: 51.6 us
  Pallas kernels  50.2 us (97%)
  local copies, waits for them, and re-layouts  1.33 us (3%)
    pallas_call x1, Pallas kernels, shards(): pl.pallas_call(kernel, out_shape=jax.ShapeDtypeStruct((3, 1024), F32), in...  50.2 us
    unnamed x1, local copies, waits for them, and re-layouts  1.33 us

profile of v1, /device:TPU:1, one launch (start us, length us, event | category | flops | bytes accessed | tf_op | source)
XLA Modules:
  0.0 51.6 jit_solution(50556063202129781)
XLA Ops:
  0.0 50.2 %contact_residual.1 = f32[3,1024]{1,0:T(4,128)} custom-call(bf16[8,64,64]{2,1,0:T(8,128)(2,1)} %refs_0_.1, bf16[8,64]{1,0:T(8,128)(2,1)} %refs_1_.1, s32[1,2048]{1,0:T(1,128)} %bitcast.4, bf16[64,2048]{1,0:T(8,128)(2,1)} %refs_3_.1, s32[1,2048]{1,0:T(1,128)} %bitcast.5, f32[1,2048]{1,0:T(1,128)} %bitcast.6, s32[4,2048]{1,0:T(4,128)} %refs_6_.1, ...), custom_call_target="tpu_custom_call" | custom-call | tf_op jit(solution)/shard_map/contact_residual/pallas_call | solution.py:447
  50.3 1.3 %copy.14 = f32[3,1024]{1,0:T(4,128)} copy(f32[3,1024]{1,0:T(4,128)} %contact_residual.1) | data formatting | bytes 24576

commit v2 on v1

--- a/solution.py
+++ b/solution.py
@@ -179,12 +179,6 @@
     for k in RING:
         d = 1 if k in (0, 1, 2, 3) else -1
         add(f"y{k}", ("x", d), ("one", -d, k), B, (f"x{k}" + sign(d),))
-    add("s0", ("s", 1), ("z_all", 0, 0), B, tuple(q for k in RING for q in z_arrivals(k)))
-    add("s-1", ("s", 1), ("z_all", -1, 0), B, tuple(f"x{k}+" for k in RING))
-    add("s1", ("s", 1), ("z_all", 1, 0), B, tuple(f"x{k}-" for k in RING))
-    add("sa", ("s", 1), ("all", 0, 0), A, a_line + tuple(q for k in RING for q in az_arrivals(k)))
-    for k in RING:
-        add(f"sy{k}", ("s", 1), ("one", 2, k), B, (f"y{k}",))
     return t
 
 
@@ -200,24 +194,20 @@
     return tuple("a" + q for q in z_arrivals(k))
 
 
-def needed(core, rx, k):
-    if core:
-        return {"sa"} | ({f"sy{k}"} if rx == 2 else {f"s{rx}"})
+def needed(rx, k):
     part_a = set(az_arrivals(k)) if k else set({0: (), -1: ("ax+",), 1: ("ax-",), 2: ("a2",)}[rx])
     part_b = set(z_arrivals(k)) if rx == 0 else {{-1: f"x{k}+", 1: f"x{k}-", 2: f"y{k}"}[rx]}
     return part_a | part_b
 
 
 EXPECTED = {
-    "z1": 6.0, "z2": 7.0, "ax": 6.2, "a2": 6.6, "x0": 8.0, "z3": 10.0, "z4": 11.0, "az1": 10.2, "az2": 11.2, "x-1": 9.0, "x1": 9.0,
-    "x-2": 12.0, "x2": 12.0, "az3": 14.0, "az4": 15.0, "x-3": 15.0, "x3": 15.0, "x4": 16.0, "y0": 12.5, "y-1": 14.5, "y1": 14.5,
-    "y-2": 17.0, "y2": 17.0, "y-3": 20.0, "y3": 20.0, "y4": 21.0, "s0": 13.0, "sa": 16.5, "s-1": 18.0, "s1": 18.0,
+    "z1": 9.0, "z2": 10.5, "ax": 7.5, "a2": 8.5, "x0": 9.0, "z3": 13.5, "z4": 14.5, "az1": 12.5, "az2": 13.5, "x-1": 12.6, "x1": 12.6,
+    "x-2": 14.6, "x2": 14.8, "az3": 17.0, "az4": 17.5, "x-3": 18.0, "x3": 18.2, "x4": 20.0, "y0": 12.8, "y-1": 16.0, "y1": 16.2,
+    "y-2": 19.0, "y2": 19.2, "y-3": 22.0, "y3": 22.2, "y4": 23.5,
 }
 
 
 def expected(name):
-    if name.startswith("sy"):
-        return EXPECTED[name[1:]] + 2.0
     return EXPECTED[name.rstrip("+-") if name not in EXPECTED else name]
 
 
@@ -265,16 +255,12 @@
         kind, rx, rz = spec
         x, z, r = (x + rx + NX) % NX, (z + rz + NZ) % NZ, pl.ds(*rows)
         if kind == "x_all":
-            return self.blocks.at[:, z, core, r]
+            return self.blocks.at[:, z, r]
         if kind == "x_low":
-            return self.blocks.at[pl.ds(0, 2), z, core, r]
+            return self.blocks.at[pl.ds(0, 2), z, r]
         if kind == "x_high":
-            return self.blocks.at[pl.ds(2, 2), z, core, r]
-        if kind == "z_all":
-            return self.blocks.at[x, :, core, r]
-        if kind == "all":
-            return self.blocks.at[:, :, core, r]
-        return self.blocks.at[x, z, core, r]
+            return self.blocks.at[pl.ds(2, 2), z, r]
+        return self.blocks.at[x, z, r]
 
     def copy(self, i, arriving=False):
         _, direction, spec, rows, after = self.table[i]
@@ -305,22 +291,23 @@
 VM = pl.BlockSpec(memory_space=pltpu.VMEM)
 
 
-def owner_force(x, z, core, table, blocks_ref, sorted_ref, segment_ref):
+def owner_force(x, z, core, faces, blocks_ref):
     owner = (x * NZ + z) * 2 + core
-    first = jnp.clip(table[0, owner], 0, sorted_ref.shape[0] - CAP)
-    offset = blocks_ref[x, z, core, 64:72, :].astype(F32)[0:1]
-    rows = sorted_ref[pl.ds(first, CAP), :].astype(BF16)
-    masks = segment_masks(segment_ref[pl.ds(first, CAP), :])
-    every = dot(rows[:, 0:64], blocks_ref[x, z, core, 0:64, :])
-    gap = jnp.zeros((CAP, 128), F32)
+    offset = blocks_ref[x, z, 64:72, :].astype(F32)[0:1]
+    at = [pl.ds(jnp.clip(table[0, owner], 0, sorted_ref.shape[0] - CAP), CAP) for sorted_ref, _, table, _ in faces]
+    rows = [f[0][a, :].astype(BF16) for f, a in zip(faces, at)]
+    masks = segment_masks(jnp.concatenate([f[1][a, :] for f, a in zip(faces, at)], axis=0))
+    every = dot(jnp.concatenate(rows, axis=0)[:, 0:64], blocks_ref[x, z, 0:64, :])
+    gap = jnp.zeros((len(faces) * CAP, 128), F32)
     for p in range(4):
-        at = slice(128 * p, 128 * p + 128)
-        gap = jnp.where(masks[p], every[:, at] - offset[:, at], gap)
+        cut = slice(128 * p, 128 * p + 128)
+        gap = jnp.where(masks[p], every[:, cut] - offset[:, cut], gap)
     traction = jnp.maximum(-gap, 0.0) + jnp.log(1.0 + jnp.exp(-jnp.abs(gap)))
     parts = [jnp.concatenate([jnp.where(m, part.astype(F32), 0.0) for m in masks], axis=1) for part in split(traction)]
-    force = dot_nt(jnp.concatenate(parts, axis=0).astype(BF16), blocks_ref[x, z, core, 0:64, :])
-    held = jnp.where(iota((1, CAP), 1) < table[1, owner], 1.0, 0.0)
-    return rows, (force[:CAP] + force[CAP:]).astype(BF16), held
+    force = dot_nt(jnp.concatenate(parts, axis=0).astype(BF16), blocks_ref[x, z, 0:64, :])
+    force = (force[: len(faces) * CAP] + force[len(faces) * CAP :]).astype(BF16)
+    held = [jnp.where(iota((1, CAP), 1) < f[2][1, owner], 1.0, 0.0) for f in faces]
+    return [(rows[k], force[CAP * k : CAP * k + CAP], held[k]) for k in range(len(faces))]
 
 
 def spread_faces(found, shape_ref, total_ref):
@@ -336,13 +323,15 @@
 
 def kernel(*refs):
     inputs, out_ref, buffers = refs[:12], refs[12], refs[13:25]
-    blocks_ref, sorted_ref, segment_ref, mine, low_ref, total_ref, table_ref, rims, came, table = refs[25:35]
-    load_sem, own_sem, send_sem, recv_sem, rim_send, rim_recv = refs[35:]
+    blocks_ref, sorted_ref, segment_ref, sorted_two, segment_two, mine, low_ref, total_ref, total_two, total_came = refs[25:35]
+    table_ref, table_came, rims, came, table, table_two = refs[35:41]
+    load_sem, own_sem, send_sem, recv_sem, rim_send, rim_recv, share_send, share_recv = refs[41:]
     slabs = lax.axis_size("slab")
     gather = Gather(mine, blocks_ref, send_sem, recv_sem)
     v, y = lax.axis_index("vol"), gather.y
     peers = ((v, (y + 1) % slabs), (v, (y + slabs - 1) % slabs))
-    enter = gather.greet(peers)
+    twin = (v + 1 - 2 * gather.c, y)
+    enter = gather.greet(peers + (twin,))
     loads = [pltpu.make_async_copy(s, d, load_sem.at[k]) for k, (s, d) in enumerate(zip(inputs, buffers))]
     for load in loads:
         load.start()
@@ -372,48 +361,73 @@
     segment_ref[2048:, :] = jnp.zeros((CAP, 128), F32)
     own.wait()
     to_smem.wait()
-
-    def owners(core, rx, ks):
+    for k in range(8):
+        permute_rows(k, row, content, sorted_ref, segment_ref)
+    shared = [
+        pltpu.make_async_remote_copy(
+            src_ref=source, dst_ref=target, send_sem=share_send.at[k], recv_sem=share_recv.at[k], device_id=twin, device_id_type=MESH)
+        for k, (source, target) in enumerate(
+            ((table_ref, table_came), (sorted_ref, sorted_two), (segment_ref, segment_two), (total_two, total_came)))
+    ]
+    for copy in shared[:3]:
+        copy.start()
+    total_two[...] = jnp.zeros_like(total_two)
+    faces = ((sorted_ref, segment_ref, table, total_ref), (sorted_two, segment_two, table_two, total_two))
+
+    def receive():
+        for copy in shared[:3]:
+            copy.wait()
+        move = pltpu.make_async_copy(table_came, table_two, own_sem.at[1])
+        move.start()
+        move.wait()
+
+    def owners(rx, ks):
         found = []
         for k in ks:
             z = (gather.z + k + NZ) % NZ
             x = (gather.x + rx + NX) % NX
-            c = 1 - gather.c if core else gather.c
-            found.append(owner_force(x, z, c, table, blocks_ref, sorted_ref, segment_ref))
-        spread_faces(found, shape, total_ref)
-
-    work = [(set(), lambda k=k: permute_rows(k, row, content, sorted_ref, segment_ref)) for k in range(8)]
-    early = {"z1+", "z1-", "z2+", "z2-", "ax+", "ax-", "a2", "x0+", "x0-"}
-    late = {"z3+", "z3-", "z4+", "z4-", "az1+", "az1-", "az2+", "az2-"}
-    work.append((early, lambda: elements(node[...], connect[...], stiffness[...], matrix[...], total_ref, low_ref)))
-    for core in (0, 1):
-        for rx in (0, -1, 1, 2):
-            for ks in ((0, -1, 1, -2), (2, -3, 3, 4)):
-                need = set().union(*[needed(core, rx, k) for k in ks]) | late
-                work.append((need, lambda core=core, rx=rx, ks=ks: owners(core, rx, ks)))
+            found.append(owner_force(x, z, gather.c, faces, blocks_ref))
+        for k in range(2):
+            spread_faces([f[k] for f in found], shape, faces[k][3])
+
+    early = {"z1+", "z1-", "z2+", "z2-", "ax+", "ax-", "a2"}
+    work = [(early, ELEMENTS_US, lambda: elements(node[...], connect[...], stiffness[...], matrix[...], total_ref, low_ref))]
+    work.append((early, 0.3, receive))
+    for rx in (0, -1, 1, 2):
+        for ks in ((0, -1, 1, -2), (2, -3, 3, 4)):
+            need = set().union(*[needed(rx, k) for k in ks]) | early
+            work.append((need, OWNERS_US, lambda rx=rx, ks=ks: owners(rx, ks)))
     seen = set()
 
-    def do(budget):
-        for _ in range(budget):
-            for i, (need, piece) in enumerate(work):
-                if need <= seen:
+    def do(room):
+        used = 0.0
+        while True:
+            for i, (need, cost, piece) in enumerate(work):
+                if need <= seen and used + cost <= room:
                     work.pop(i)
                     piece()
+                    used += cost
                     break
             else:
-                return
-
-    do(BEFORE_FIRST_WAIT)
+                return used
+
+    clock = FIRST_WAIT_US
     for e in gather.order[first_wait:]:
         if e >= 0:
             gather.copy(e).start()
+            clock += 0.05
             continue
+        due = expected(gather.table[~e][0])
+        clock += do(due + SLACK_US - clock)
         gather.copy(~e, True).wait_recv()
+        clock = max(clock, due) + 0.05
         seen.add(gather.table[~e][0])
-        do(1)
-    do(len(work))
+    do(1e9)
     assert not work
+    shared[3].start()
     gather.leave()
+    shared[3].wait()
+    total_ref[...] += total_came[...]
     total = total_ref[...]
     grids = [total[16 * c : 16 * c + 8] + total[16 * c + 8 : 16 * c + 16] for c in range(3)]
     for c in range(3):
@@ -437,7 +451,7 @@
             out_ref[c : c + 1, 128 * h : 128 * h + 128] = line
 
 
-BEFORE_FIRST_WAIT = 8
+FIRST_WAIT_US, ELEMENTS_US, OWNERS_US, SLACK_US = 9.0, 2.5, 1.3, 100.0
 
 
 def shards(face_disp, contact_owner, segment, face_area, face_nodes, mortar_blocks, gap_offset, shape_table, node_disp, stiffness, connect, elem_matrix):
@@ -451,15 +465,21 @@
         out_specs=VM,
         scratch_shapes=[pltpu.VMEM(a.shape, a.dtype) for a in arrays]
         + [
-            pltpu.VMEM((NX, NZ, 2, BLOCK, 512), BF16),
+            pltpu.VMEM((NX, NZ, BLOCK, 512), BF16),
+            pltpu.VMEM((2048 + CAP, 128), F32),
+            pltpu.VMEM((2048 + CAP, 128), F32),
             pltpu.VMEM((2048 + CAP, 128), F32),
             pltpu.VMEM((2048 + CAP, 128), F32),
             pltpu.VMEM((BLOCK, 512), BF16),
             pltpu.VMEM((8, 128, 1024), BF16),
             pltpu.VMEM((48, 128), F32),
+            pltpu.VMEM((48, 128), F32),
+            pltpu.VMEM((48, 128), F32),
+            pltpu.VMEM((8, 128), I32),
             pltpu.VMEM((8, 128), I32),
             pltpu.VMEM((24, 128), F32),
             pltpu.VMEM((2, 24, 128), F32),
+            pltpu.SMEM((8, 128), I32),
             pltpu.SMEM((8, 128), I32),
             pltpu.SemaphoreType.DMA((12,)),
             pltpu.SemaphoreType.DMA((2,)),
@@ -467,6 +487,8 @@
             pltpu.SemaphoreType.DMA((COPIES,)),
             pltpu.SemaphoreType.DMA((2,)),
             pltpu.SemaphoreType.DMA((2,)),
+            pltpu.SemaphoreType.DMA((4,)),
+            pltpu.SemaphoreType.DMA((4,)),
         ],
         compiler_params=pltpu.CompilerParams(collective_id=0, has_side_effects=True, vmem_limit_bytes=60 << 20),
         name="contact_residual",

time: 51.8 us -> 49 us (0.946)
  Pallas kernels: 50.2 us -> 47.4 us
    pallas_call x1, Pallas kernels: 50.2 us -> 47.4 us  [shards(): pl.pallas_call(kernel, out_shape=jax.ShapeDtypeStruct((3, 1024), F32), in...]
where the time goes in v2:
time: 49 us; the launch traced here: 48.8 us
  Pallas kernels  47.4 us (97%)
  local copies, waits for them, and re-layouts  1.33 us (3%)
    pallas_call x1, Pallas kernels, shards(): pl.pallas_call(kernel, out_shape=jax.ShapeDtypeStruct((3, 1024), F32), in...  47.4 us
    unnamed x1, local copies, waits for them, and re-layouts  1.33 us

profile of v2, /device:TPU:1, one launch (start us, length us, event | category | flops | bytes accessed | tf_op | source)
XLA Modules:
  0.0 48.8 jit_solution(7942514060776030745)
XLA Ops:
  0.0 47.4 %contact_residual.1 = f32[3,1024]{1,0:T(4,128)} custom-call(bf16[8,64,64]{2,1,0:T(8,128)(2,1)} %refs_0_.1, bf16[8,64]{1,0:T(8,128)(2,1)} %refs_1_.1, s32[1,2048]{1,0:T(1,128)} %bitcast.4, bf16[64,2048]{1,0:T(8,128)(2,1)} %refs_3_.1, s32[1,2048]{1,0:T(1,128)} %bitcast.5, f32[1,2048]{1,0:T(1,128)} %bitcast.6, s32[4,2048]{1,0:T(4,128)} %refs_6_.1, ...), custom_call_target="tpu_custom_call" | custom-call | tf_op jit(solution)/shard_map/contact_residual/pallas_call | solution.py:461
  47.4 1.3 %copy.14 = f32[3,1024]{1,0:T(4,128)} copy(f32[3,1024]{1,0:T(4,128)} %contact_residual.1) | data formatting | bytes 24576
